TPU v7x, 256 devices: a whole 4x4x8 slice. The times are simulated.
256 devices in a mesh: queue: 16 (over z_hi, y, core), seq: 16 (over z_lo, x).
Axes of the slice: x: 4, y: 4, z: 8 (z_hi: 2, z_lo: 4; z = z_hi * 4 + z_lo), core: 2. Of those that a mesh axis runs over, the one named last changes fastest.
Arguments:
- latents: float32 [64, 16, 2048], P('queue', None, 'seq'), may hold values from -6 to 6
- step_index: int32 [64], P('queue'), may hold values from 0 to 29, as said below
- levels: float32 [31], replicated, may hold values from 0 to 1, as said below
- modulation: float32 [30, 5, 1152], replicated, may hold values from -4 to 4
- embed_weight: bfloat16 [16, 1152], replicated, may hold values from -1.5 to 1.5
- position: bfloat16 [2048, 1152], P('seq'), may hold values from -3 to 3
- qkv_weight: bfloat16 [1152, 3456], replicated, may hold values from -0.1875 to 0.1875
- q_gain: float32 [72], replicated, may hold values from 1 to 2.5
- k_gain: float32 [72], replicated, may hold values from 1 to 2.5
- text_kv: bfloat16 [2, 128, 1152], P(None, None, 'seq'), may hold values from -6 to 6
- out_weight: bfloat16 [1152, 1152], replicated, may hold values from -0.1875 to 0.1875
- final_weight: bfloat16 [1152, 16], replicated, may hold values from -0.1875 to 0.1875
- new_noise: float32 [16, 2048], P(None, 'seq'), may hold values from -6 to 6
Outputs:
- advanced: float32 [64, 16, 2048], P('queue', None, 'seq')
- velocity: float32 [64, 16, 2048], P('queue', None, 'seq')
Inputs may be any that keep to these rules, and one draw needn't show every extreme that they name: `step_index`: frame 0 has index 0 and the last frame 30 - 1; frame j otherwise has j * 30 // 64 or one more, at most 29. levels rise strictly from exactly 0 at index 0 to exactly 1 at index 30.
All inputs are finite; a program needn't handle non-finite values.
Results may differ from a plain program's by a relative error of at most 0.0044.
Values may be sent and summed in bfloat16 or wider, within the bound.
A program may use at most 128 MiB of HBM per device.

v0:
```python
import math

import jax
import jax.numpy as jnp
from jax import lax
from jax.sharding import PartitionSpec as P

EPSILON = 1e-06


def exchange_in_groups(shard, axis, split_dim, concat_dim, work, item_dim, out_dim):

    def moved(group):
        return lax.all_to_all(group, axis, split_axis=split_dim, concat_axis=concat_dim, tiled=True)

    items = jax.tree.leaves(shard)[0].shape[item_dim]
    ends = [items * k // 2 for k in range(2 + 1)] if items % 2 == 0 else [0, items]
    groups = [
        jax.tree.map(lambda a: lax.slice_in_dim(a, low, high, axis=item_dim), shard)
        for low, high in zip(ends, ends[1:])
    ]
    arrived = [moved(group) for group in groups]
    made = [work(group) for group in arrived]
    return jax.tree.map(lambda *parts: jnp.concatenate(parts, axis=out_dim), *made)


def passed_along(block, axis, distance):
    devices = range(lax.axis_size(axis))
    route = [(i - distance, i) for i in devices if i - distance in devices]
    return lax.ppermute(block, axis, route)


def layer_norm(values):
    center = values - jnp.mean(values, axis=-1, keepdims=True)
    return center * lax.rsqrt(jnp.mean(center * center, axis=-1, keepdims=True) + EPSILON)


def head_norm(values, gain_vector):
    widened = values.astype(jnp.float32)
    scaled = (
        widened
        * lax.rsqrt(jnp.mean(widened * widened, axis=-1, keepdims=True) + EPSILON)
        * gain_vector
    )
    return scaled.astype(jnp.bfloat16)


def text_mix(query_block, text_keys, text_values, factor):
    text_scores = (
        jnp.einsum("fqhe,khe->fhqk", query_block, text_keys, preferred_element_type=jnp.float32)
        * factor
    )
    text_weights = jnp.exp(text_scores)
    text_numerator = jnp.einsum(
        "fhqk,khe->fqhe",
        text_weights.astype(jnp.bfloat16),
        text_values,
        preferred_element_type=jnp.float32,
    )
    text_sum = jnp.moveaxis(jnp.sum(text_weights, axis=-1), 1, 2)[..., None]
    return text_numerator / text_sum


def frame_attention(queries, keys_all, values_all, text_keys, text_values):
    frame_count, token_count, head_count, head_width = queries.shape
    factor = 1.0 / math.sqrt(head_width)
    block_rows = 512
    block_count = token_count // block_rows
    grouped = jnp.moveaxis(
        queries.reshape(frame_count, block_count, block_rows, head_count, head_width), 1, 0
    )

    def one_block(query_block):
        scores = (
            jnp.einsum("fqhe,fkhe->fhqk", query_block, keys_all, preferred_element_type=jnp.float32)
            * factor
        )
        weights = jnp.exp(scores)
        numerator = jnp.einsum(
            "fhqk,fkhe->fqhe",
            weights.astype(jnp.bfloat16),
            values_all,
            preferred_element_type=jnp.float32,
        )
        weight_sum = jnp.moveaxis(jnp.sum(weights, axis=-1), 1, 2)[..., None]
        return numerator / weight_sum + text_mix(query_block, text_keys, text_values, factor)

    mixture = lax.map(one_block, grouped)
    return jnp.moveaxis(mixture, 0, 1).reshape(frame_count, token_count, head_count, head_width)


def body(
    latents,
    step_index,
    levels,
    modulation,
    embed_weight,
    position,
    qkv_weight,
    q_gain,
    k_gain,
    text_kv,
    out_weight,
    final_weight,
    new_noise,
):
    highest = lax.Precision.HIGHEST
    frame_count = latents.shape[0]
    tok_local = latents.shape[2]
    steps_count = modulation.shape[0]
    model_width = modulation.shape[2]
    head_width = q_gain.shape[0]
    select = (step_index[:, None] == jnp.arange(steps_count, dtype=jnp.int32)[None, :]).astype(
        jnp.float32
    )
    frame_mods = jnp.dot(
        select, modulation.reshape(steps_count, 5 * model_width), precision=highest
    ).reshape(frame_count, 5, 1, model_width)
    level_low = jnp.dot(select, levels[:steps_count], precision=highest)
    level_high = jnp.dot(select, levels[1:], precision=highest)
    step_size = level_high - level_low
    text_len = text_kv.shape[1]
    text_keys = head_norm(text_kv[0].reshape(text_len, -1, head_width), k_gain)
    text_values = text_kv[1].reshape(text_len, -1, head_width)
    hidden = jnp.einsum("fcn,cd->fnd", latents, embed_weight.astype(jnp.float32), precision=highest)
    hidden = hidden + position.astype(jnp.float32)[None]
    normed = (layer_norm(hidden) * (1.0 + frame_mods[:, 1]) + frame_mods[:, 0]).astype(jnp.bfloat16)
    projected = jnp.dot(
        normed.reshape(frame_count * tok_local, model_width),
        qkv_weight,
        preferred_element_type=jnp.float32,
    )
    projected = projected.astype(jnp.bfloat16).reshape(frame_count, tok_local, 3 * model_width)
    queries = projected[:, :, :model_width]
    keys_raw = projected[:, :, model_width : 2 * model_width]
    values_raw = projected[:, :, 2 * model_width :]

    def regrouped(regrouped_parts):
        query_part, key_part, value_part = regrouped_parts
        item_count, all_tokens, local_width = query_part.shape
        local_heads = local_width // head_width
        shape_four = (item_count, all_tokens, local_heads, head_width)
        mixture = frame_attention(
            head_norm(query_part.reshape(shape_four), q_gain),
            head_norm(key_part.reshape(shape_four), k_gain),
            value_part.reshape(shape_four),
            text_keys,
            text_values,
        )
        mixture = mixture.astype(jnp.bfloat16).reshape(item_count, all_tokens, local_width)
        return lax.all_to_all(mixture, "seq", split_axis=1, concat_axis=2, tiled=True)

    attention = exchange_in_groups((queries, keys_raw, values_raw), "seq", 2, 1, regrouped, 0, 0)
    branch = jnp.dot(
        attention.reshape(frame_count * tok_local, model_width),
        out_weight,
        preferred_element_type=jnp.float32,
    )
    hidden_two = hidden + frame_mods[:, 2] * branch.reshape(frame_count, tok_local, model_width)
    normed_two = (layer_norm(hidden_two) * (1.0 + frame_mods[:, 4]) + frame_mods[:, 3]).astype(
        jnp.bfloat16
    )
    velocity = jnp.einsum(
        "fnd,dc->fcn", normed_two, final_weight, preferred_element_type=jnp.float32
    )
    updated = latents + velocity * step_size[:, None, None]
    arrived = passed_along(updated[0], "queue", -1)
    at_end = lax.axis_index("queue") == lax.axis_size("queue") - 1
    arrived = jnp.where(at_end, new_noise, arrived)
    advanced = jnp.concatenate([updated[1:], arrived[None]], axis=0)
    return (advanced, velocity)


def solution(mesh):
    in_specs = (
        P("queue", None, "seq"),
        P("queue"),
        P(),
        P(),
        P(),
        P("seq", None),
        P(),
        P(),
        P(),
        P(None, None, "seq"),
        P(),
        P(),
        P(None, "seq"),
    )
    out_specs = (P("queue", None, "seq"), P("queue", None, "seq"))
    return jax.shard_map(body, mesh=mesh, in_specs=in_specs, out_specs=out_specs, check_vma=False)
```

profile of v0, /device:TPU:89, one launch (start us, length us, event | category | flops | bytes accessed | tf_op | source)
XLA Modules:
  0.0 270.8 jit_solution(1263341088654922515)
XLA Ops:
  11.0 8.4 %convolution_convert_fusion = bf16[512,3456]{1,0:T(8,128)(2,1)S(1)} fusion(bf16[512,1152]{1,0:T(8,128)(2,1)S(1)} %bitcast.357, bf16[1152,3456]{1,0:T(8,128)(2,1)} %param.23), kind=kOutput, calls=%fused_computation.62 | convolution fusion | flops 4078632960 | bytes 12681216 | tf_op jit(solution)/shard_map/dot_general | solution.py:128
  22.8 7.5 %all-to-all-start = ((bf16[2,128,1152]{1,0,2:T(2,128)(2,1)}), bf16[2,128,1152]{1,0,2:T(2,128)(2,1)S(1)}, u32[]{:S(2)}, u32[]{:S(2)}) async-start(bf16[2,128,1152]{1,0,2:T(2,128)(2,1)} %copy.109), calls=%async_computation | async-start | bytes 1179648 | tf_op jit(solution)/shard_map/all_to_all | solution.py:14
  30.3 2.9 %copy.113 = bf16[2,128,1152]{1,0,2:T(2,128)(2,1)} copy(bf16[2,128,1152]{2,1,0:T(8,128)(2,1)} %get-tuple-element.157) | data formatting | bytes 1179648
  33.2 3.0 %copy.110 = bf16[2,128,1152]{1,0,2:T(2,128)(2,1)} copy(bf16[2,128,1152]{2,1,0:T(8,128)(2,1)} %get-tuple-element.159) | data formatting | bytes 1179648
  36.2 3.0 %copy.112 = bf16[2,128,1152]{1,0,2:T(2,128)(2,1)} copy(bf16[2,128,1152]{2,1,0:T(8,128)(2,1)} %get-tuple-element.158) | data formatting | bytes 1179648
  39.2 3.0 %copy.111 = bf16[2,128,1152]{1,0,2:T(2,128)(2,1)} copy(bf16[2,128,1152]{2,1,0:T(8,128)(2,1)} %get-tuple-element.156) | data formatting | bytes 1179648
  46.3 5.8 %all-to-all-start.4 = ((bf16[2,128,1152]{1,0,2:T(2,128)(2,1)}), bf16[2,128,1152]{1,0,2:T(2,128)(2,1)}, u32[]{:S(2)}, u32[]{:S(2)}) async-start(bf16[2,128,1152]{1,0,2:T(2,128)(2,1)} %copy.112), calls=%async_computation.4 | async-start | bytes 1179648 | tf_op jit(solution)/shard_map/all_to_all | solution.py:14
  54.6 13.5 %all-to-all-done.4 = bf16[2,128,1152]{1,0,2:T(2,128)(2,1)} async-done(((bf16[2,128,1152]{1,0,2:T(2,128)(2,1)}), bf16[2,128,1152]{1,0,2:T(2,128)(2,1)}, u32[]{:S(2)}, u32[]{:S(2)}) %all-to-all-start.4) | async-done | bytes 589856 | tf_op jit(solution)/shard_map/all_to_all | solution.py:14
  68.2 4.4 %all-to-all-start.5 = ((bf16[2,128,1152]{1,0,2:T(2,128)(2,1)}), bf16[2,128,1152]{1,0,2:T(2,128)(2,1)}, u32[]{:S(2)}, u32[]{:S(2)}) async-start(bf16[2,128,1152]{1,0,2:T(2,128)(2,1)} %copy.113), calls=%async_computation.5 | async-start | bytes 1179648 | tf_op jit(solution)/shard_map/all_to_all | solution.py:14
  79.3 9.1 %all-to-all-done.5 = bf16[2,128,1152]{1,0,2:T(2,128)(2,1)} async-done(((bf16[2,128,1152]{1,0,2:T(2,128)(2,1)}), bf16[2,128,1152]{1,0,2:T(2,128)(2,1)}, u32[]{:S(2)}, u32[]{:S(2)}) %all-to-all-start.5) | async-done | bytes 589856 | tf_op jit(solution)/shard_map/all_to_all | solution.py:14
  88.5 4.4 %all-to-all-start.1 = ((bf16[2,128,1152]{1,0,2:T(2,128)(2,1)}), bf16[2,128,1152]{1,0,2:T(2,128)(2,1)S(1)}, u32[]{:S(2)}, u32[]{:S(2)}) async-start(bf16[2,128,1152]{1,0,2:T(2,128)(2,1)} %copy.110), calls=%async_computation.1 | async-start | bytes 1179648 | tf_op jit(solution)/shard_map/all_to_all | solution.py:14
  108.5 6.0 %all-to-all-start.2 = ((bf16[2,128,1152]{1,0,2:T(2,128)(2,1)}), bf16[2,128,1152]{1,0,2:T(2,128)(2,1)}, u32[]{:S(2)}, u32[]{:S(2)}) async-start(bf16[2,128,1152]{1,0,2:T(2,128)(2,1)} %copy.111), calls=%async_computation.2 | async-start | bytes 1179648 | tf_op jit(solution)/shard_map/all_to_all | solution.py:14
  133.1 7.0 %all-to-all-start.6 = ((bf16[2,128,1152]{1,0,2:T(2,128)(2,1)}), bf16[2,128,1152]{1,0,2:T(2,128)(2,1)}, u32[]{:S(2)}, u32[]{:S(2)}) async-start(bf16[2,128,1152]{1,0,2:T(2,128)(2,1)} %copy.114), calls=%async_computation.6 | async-start | bytes 1179648 | tf_op jit(solution)/shard_map/all_to_all | solution.py:14
  143.5 3.0 %multiply_convert_fusion.2 = (bf16[2,2048,1,72]{1,3,0,2:T(8,128)(2,1)}, bf16[2,2048,1,72]{1,3,0,2:T(8,128)(2,1)}) fusion(f32[2,2048,1,72]{1,3,0,2:T(8,128)} %reshape.503, f32[72]{0:T(128)S(1)} %copy-done.7, f32[2,2048]{1,0:T(2,128)S(1)} %get-tuple-element.178, f32[2,2048,1,72]{1,3,0,2:T(8,128)} %reshape.506, f32[2,2048]{1,0:T(2,128)S(1)} %get-tuple-element.177), kind=kLoop, calls=%fused_computation.77 | loop fusion | flops 1769472 | bytes 3572000 | tf_op jit(solution)/shard_map/convert_element_type | solution.py:45
  147.4 25.2 %while.20 = (s32[]{:T(128)}, bf16[4,2,512,1,72]{2,4,1,3,0:T(8,128)(2,1)}, bf16[4,2,512,1,72]{2,4,1,3,0:T(8,128)(2,1)}, bf16[2,2048,1,72]{1,3,0,2:T(8,128)(2,1)},...) while((s32[]{:T(128)}, ...), condition=%wide.region_8.9_spmd, body=%wide.region_5.8_spmd.sunk | while | flops 650729472 | bytes 19715668 | solution.py:88
  172.6 3.6 %copy.101 = bf16[2,4,512,1,72]{4,0,2,1,3:T(2,128)(2,1)} copy(bf16[2,4,512,1,72]{2,4,0,3,1:T(8,128)(2,1)} %bitcast.266) | data formatting | bytes 1179648 | tf_op jit(solution)/shard_map/convert_element_type | solution.py:150
  178.1 7.0 %all-to-all-start.3 = ((bf16[2,2048,72]{2,0,1:T(2,128)(2,1)}), bf16[2,2048,72]{2,0,1:T(2,128)(2,1)}, u32[]{:S(2)}, u32[]{:S(2)}) async-start(bf16[2,2048,72]{2,0,1:T(2,128)(2,1)} %bitcast.349), calls=%async_computation.3 | async-start | bytes 2097152 | tf_op jit(solution)/shard_map/all_to_all | solution.py:151
  189.3 25.1 %while.21 = (s32[]{:T(128)}, bf16[4,2,512,1,72]{2,4,1,3,0:T(8,128)(2,1)}, bf16[4,2,512,1,72]{2,4,1,3,0:T(8,128)(2,1)}, bf16[2,2048,1,72]{1,3,0,2:T(8,128)(2,1)},...) while((s32[]{:T(128)}, ...), condition=%wide.region_14.15_spmd, body=%wide.region_11.14_spmd.sunk | while | flops 650729472 | bytes 19715668 | solution.py:88
  214.5 3.6 %copy.104 = bf16[2,4,512,1,72]{4,0,2,1,3:T(2,128)(2,1)} copy(bf16[2,4,512,1,72]{2,4,0,3,1:T(8,128)(2,1)} %bitcast.265) | data formatting | bytes 1179648 | tf_op jit(solution)/shard_map/convert_element_type | solution.py:150
  218.1 7.0 %all-to-all-start.7 = ((bf16[2,2048,72]{2,0,1:T(2,128)(2,1)}), bf16[2,2048,72]{2,0,1:T(2,128)(2,1)}, u32[]{:S(2)}, u32[]{:S(2)}) async-start(bf16[2,2048,72]{2,0,1:T(2,128)(2,1)} %bitcast.350), calls=%async_computation.7 | async-start | bytes 2097152 | tf_op jit(solution)/shard_map/all_to_all | solution.py:151
  229.0 20.6 %all-to-all-done.7 = bf16[2,2048,72]{2,0,1:T(2,128)(2,1)} async-done(((bf16[2,2048,72]{2,0,1:T(2,128)(2,1)}), bf16[2,2048,72]{2,0,1:T(2,128)(2,1)}, u32[]{:S(2)}, u32[]{:S(2)}) %all-to-all-start.7) | async-done | bytes 589856 | tf_op jit(solution)/shard_map/all_to_all | solution.py:151
  253.1 4.0 %fusion.102 = (f32[4,128]{1,0:T(4,128)S(1)}, f32[4,128,1152]{2,1,0:T(8,128)S(1)}) fusion(f32[4,128,1152]{2,1,0:T(8,128)} %copy-done.1, bf16[1152,1152]{1,0:T(8,128)(2,1)S(1)} %copy-done, bf16[2,128,1152]{2,1,0:T(8,128)(2,1)} %copy.98, bf16[2,128,1152]{2,1,0:T(8,128)(2,1)} %copy.97, f32[4,1152]{1,0:T(4,128)S(1)} %get-tuple-element.166), kind=kOutput, calls=%fused_computation.139 | convolution fusion | flops 1361313280 | bytes 8572928 | tf_op jit(solution)/shard_map/dot_general | solution.py:154
  259.2 4.5 %collective-permute-start = (f32[16,128]{1,0:T(8,128)S(1)}, f32[16,128]{1,0:T(8,128)S(1)}, u32[]{:S(2)}, u32[]{:S(2)}) collective-permute-start(f32[16,128]{1,0:T(8,128)S(1)} %slice_bitcast_fusion.4), channel_id=1, source_target_pairs={{16,0},{32,16},{48,32},{64,48},{80,64},{96,80},{112,96},{128,112},... | collective-permute-start | bytes 24584 | tf_op jit(solution)/shard_map/ppermute | solution.py:30
  263.7 6.5 %collective-permute-done = f32[16,128]{1,0:T(8,128)S(1)} collective-permute-done((f32[16,128]{1,0:T(8,128)S(1)}, f32[16,128]{1,0:T(8,128)S(1)}, u32[]{:S(2)}, u32[]{:S(2)}) %collective-permute-start) | collective-permute-done | bytes 8224 | tf_op jit(solution)/shard_map/ppermute | solution.py:30
  (132 shorter events, 132.1 us)
Async XLA Ops:
  0.6 252.5 %copy-start = (bf16[1152,1152]{1,0:T(8,128)(2,1)S(1)}, bf16[1152,1152]{1,0:T(8,128)(2,1)}, u32[]{:S(2)}) copy-start(bf16[1152,1152]{1,0:T(8,128)(2,1)} %param.27) | copy-start | bytes 7962628
  1.8 2.6 copy-start.3
  4.0 1.4 copy-start.1
  5.5 1.3 copy-start.8
  22.8 23.5 %all-to-all-start = ((bf16[2,128,1152]{1,0,2:T(2,128)(2,1)}), bf16[2,128,1152]{1,0,2:T(2,128)(2,1)S(1)}, u32[]{:S(2)}, u32[]{:S(2)}) async-start(bf16[2,128,1152]{1,0,2:T(2,128)(2,1)} %copy.109), calls=%async_computation | async-start | bytes 1179648 | tf_op jit(solution)/shard_map/all_to_all | solution.py:14
  33.2 11.8 %copy-start.4 = (bf16[2,128,72]{1,2,0:T(8,128)(2,1)S(1)}, bf16[2,128,72]{1,2,0:T(8,128)(2,1)}, u32[]{:S(2)}) copy-start(bf16[2,128,72]{1,2,0:T(8,128)(2,1)} %param.26) | copy-start | bytes 110596
  36.2 15.9 %copy-start.7 = (f32[72]{0:T(128)S(1)}, f32[72]{0:T(128)}, u32[]{:S(2)}) copy-start(f32[72]{0:T(128)} %param.25) | copy-start | bytes 868
  46.3 21.9 %all-to-all-start.4 = ((bf16[2,128,1152]{1,0,2:T(2,128)(2,1)}), bf16[2,128,1152]{1,0,2:T(2,128)(2,1)}, u32[]{:S(2)}, u32[]{:S(2)}) async-start(bf16[2,128,1152]{1,0,2:T(2,128)(2,1)} %copy.112), calls=%async_computation.4 | async-start | bytes 1179648 | tf_op jit(solution)/shard_map/all_to_all | solution.py:14
  68.2 20.3 %all-to-all-start.5 = ((bf16[2,128,1152]{1,0,2:T(2,128)(2,1)}), bf16[2,128,1152]{1,0,2:T(2,128)(2,1)}, u32[]{:S(2)}, u32[]{:S(2)}) async-start(bf16[2,128,1152]{1,0,2:T(2,128)(2,1)} %copy.113), calls=%async_computation.5 | async-start | bytes 1179648 | tf_op jit(solution)/shard_map/all_to_all | solution.py:14
  88.5 20.0 %all-to-all-start.1 = ((bf16[2,128,1152]{1,0,2:T(2,128)(2,1)}), bf16[2,128,1152]{1,0,2:T(2,128)(2,1)S(1)}, u32[]{:S(2)}, u32[]{:S(2)}) async-start(bf16[2,128,1152]{1,0,2:T(2,128)(2,1)} %copy.110), calls=%async_computation.1 | async-start | bytes 1179648 | tf_op jit(solution)/shard_map/all_to_all | solution.py:14
  105.3 9.3 %copy-start.9 = (f32[72]{0:T(128)S(1)}, f32[72]{0:T(128)}, u32[]{:S(2)}) copy-start(f32[72]{0:T(128)} %param.24) | copy-start | bytes 868
  108.5 24.7 %all-to-all-start.2 = ((bf16[2,128,1152]{1,0,2:T(2,128)(2,1)}), bf16[2,128,1152]{1,0,2:T(2,128)(2,1)}, u32[]{:S(2)}, u32[]{:S(2)}) async-start(bf16[2,128,1152]{1,0,2:T(2,128)(2,1)} %copy.111), calls=%async_computation.2 | async-start | bytes 1179648 | tf_op jit(solution)/shard_map/all_to_all | solution.py:14
  114.5 1.3 copy-start.2
  133.1 45.0 %all-to-all-start.6 = ((bf16[2,128,1152]{1,0,2:T(2,128)(2,1)}), bf16[2,128,1152]{1,0,2:T(2,128)(2,1)}, u32[]{:S(2)}, u32[]{:S(2)}) async-start(bf16[2,128,1152]{1,0,2:T(2,128)(2,1)} %copy.114), calls=%async_computation.6 | async-start | bytes 1179648 | tf_op jit(solution)/shard_map/all_to_all | solution.py:14
  178.1 39.9 %all-to-all-start.3 = ((bf16[2,2048,72]{2,0,1:T(2,128)(2,1)}), bf16[2,2048,72]{2,0,1:T(2,128)(2,1)}, u32[]{:S(2)}, u32[]{:S(2)}) async-start(bf16[2,2048,72]{2,0,1:T(2,128)(2,1)} %bitcast.349), calls=%async_computation.3 | async-start | bytes 2097152 | tf_op jit(solution)/shard_map/all_to_all | solution.py:151
  214.5 10.6 %copy-start.11 = (f32[31]{0:T(128)S(1)}, f32[31]{0:T(128)}, u32[]{:S(2)}) copy-start(f32[31]{0:T(128)} %param.19) | copy-start | bytes 376
  218.1 31.5 %all-to-all-start.7 = ((bf16[2,2048,72]{2,0,1:T(2,128)(2,1)}), bf16[2,2048,72]{2,0,1:T(2,128)(2,1)}, u32[]{:S(2)}, u32[]{:S(2)}) async-start(bf16[2,2048,72]{2,0,1:T(2,128)(2,1)} %bitcast.350), calls=%async_computation.7 | async-start | bytes 2097152 | tf_op jit(solution)/shard_map/all_to_all | solution.py:151
  257.1 0.8 copy-start.5
  257.1 0.8 copy-start.10
  257.1 13.0 %copy-start.6 = (f32[16,128]{1,0:T(8,128)S(1)}, f32[16,128]{1,0:T(8,128)}, u32[]{:S(2)}) copy-start(f32[16,128]{1,0:T(8,128)} %param.29) | copy-start | bytes 24580
  259.2 11.0 %collective-permute-start = (f32[16,128]{1,0:T(8,128)S(1)}, f32[16,128]{1,0:T(8,128)S(1)}, u32[]{:S(2)}, u32[]{:S(2)}) collective-permute-start(f32[16,128]{1,0:T(8,128)S(1)} %slice_bitcast_fusion.4), channel_id=1, source_target_pairs={{16,0},{32,16},{48,32},{64,48},{80,64},{96,80},{112,96},{128,112},... | collective-permute-start | bytes 24584 | tf_op jit(solution)/shard_map/ppermute | solution.py:30
where the time goes:
time: 273 us; the launch traced here: 271 us
  matrix products  68.2 us (25%)
  local copies, waits for them, and re-layouts  67.7 us (25%)
  starting transfers between devices  53.4 us (20%)
  waiting for transfers between devices  51.9 us (19%)
  other arithmetic  28.6 us (10%)
    all_to_all x6, starting transfers between devices, moved(): lax.all_to_all(group, axis, split_axis=split_dim, concat_axis=concat_dim,...  35 us
    all_to_all x6, waiting for transfers between devices, moved(): lax.all_to_all(group, axis, split_axis=split_dim, concat_axis=concat_dim,...  24.7 us
    dot_general x8, matrix products, one_block(): jnp.einsum('fqhe,fkhe->fhqk', query_block, keys_all, preferred_element_ty...  22.2 us
    all_to_all x2, waiting for transfers between devices, regrouped(): lax.all_to_all(mixture, 'seq', split_axis=1, concat_axis=2, tiled=True)  20.6 us
    unnamed x33, local copies, waits for them, and re-layouts  19.2 us
    convert_element_type x8, local copies, waits for them, and re-layouts, head_norm(): widened = values.astype(jnp.float32)  18.9 us
    all_to_all x2, starting transfers between devices, regrouped(): lax.all_to_all(mixture, 'seq', split_axis=1, concat_axis=2, tiled=True)  13.9 us
    dot_general x8, matrix products, one_block(): jnp.einsum('fhqk,fkhe->fqhe', weights.astype(jnp.bfloat16), values_all, p...  11.5 us
  transfers between devices with their start and end apart: 9, of which 6 were waited for; matrix products, arithmetic and copies ran while one was open for 48% of the time, Pallas kernels for 0%

commit v1 on v0

v1 whole, which is shorter than its diff:
```python
import functools
import math

import jax
import jax.numpy as jnp
from jax import lax
from jax.experimental import pallas as pl
from jax.experimental.pallas import tpu as pltpu
from jax.sharding import PartitionSpec as P

F32, BF = jnp.float32, jnp.bfloat16
MESH = pl.DeviceIdType.MESH
EPS = 1e-6
D, H, HD, C, TXT, HP = 1152, 16, 72, 16, 128, 80
ROWS = TXT + 16
CUT = 64
PARTS = ((0, CUT), (CUT, ROWS - CUT))


def nn(a, b):
    return lax.dot_general(a, b, (((1,), (0,)), ((), ())), preferred_element_type=F32)


def nt(a, b):
    return lax.dot_general(a, b, (((1,), (1,)), ((), ())), preferred_element_type=F32)


def tn(a, b):
    return lax.dot_general(a, b, (((0,), (0,)), ((), ())), preferred_element_type=F32)


def split3(x):
    a = x.astype(BF)
    r = x - a.astype(F32)
    b = r.astype(BF)
    c = (r - b.astype(F32)).astype(BF)
    return jnp.concatenate([a, b, c], axis=0)


def head_norm(rows, gain):
    ss = jnp.sum(rows * rows, axis=0, keepdims=True) * (1.0 / HD)
    return rows * lax.rsqrt(ss + EPS) * gain


def kernel(
    latx, posx, mod, levels, gains, ew, fw, noise, wqkv_hbm, wo_hbm,
    adv, vel,
    pos, lat, wqkv, wo, wt, wot, e3, mods, modsT, x, kT, vT, q, tk, tv, att, attb, hid, ubuf, vbuf,
    w_sem, own_sem, pos_send, pos_recv, lat_send, lat_recv, kv_send, kv_recv, tx_send, tx_recv,
    out_send, out_recv,
):
    qd, sq = lax.axis_index("queue"), lax.axis_index("seq")
    c = lax.rem(qd, 2)
    y = lax.rem(qd // 2, 4)
    z = (qd // 8) * 4 + sq // 4
    zl, xx = sq // 4, lax.rem(sq, 4)
    h = zl // 2
    rz = lax.rem(zl, 2)
    partner = (qd + 1 - 2 * c, sq)
    frame = sq // 2
    part = lax.rem(sq, 2)
    base = qd - c

    def at_z(step):
        zz = lax.rem(z + step + 8, 8)
        return ((zz // 4) * 8 + y * 2 + c, lax.rem(zz, 4) * 4 + xx)

    def at_x(step):
        return (qd, zl * 4 + lax.rem(xx + step, 4))

    def weights(k):
        if k < 3:
            cols = pl.ds(k * D, D)
            return pltpu.make_async_copy(wqkv_hbm.at[:, cols], wqkv.at[:, cols], w_sem.at[k])
        return pltpu.make_async_copy(wo_hbm, wo, w_sem.at[3])

    for k in range(4):
        weights(k).start()

    def rows_of(ref, color):
        low, size = PARTS[color]
        return ref.at[pl.ds(low, size), :]

    def send_block(src, slot, color, target, number):
        return pltpu.make_async_remote_copy(
            src_ref=rows_of(src, color),
            dst_ref=rows_of(pos.at[slot], color),
            send_sem=pos_send.at[number],
            recv_sem=pos_recv.at[slot, color],
            device_id=target,
            device_id_type=MESH,
        )

    def block_wait(slot, color):
        dst = rows_of(pos.at[slot], color)
        pltpu.make_async_copy(dst, dst, pos_recv.at[slot, color]).wait()

    own_slot = rz * 4 + xx
    mine = c == h
    far = 2 - 4 * lax.rem(xx, 2)

    def own_copy():
        return pltpu.make_async_copy(posx, pos.at[own_slot], own_sem.at[0])

    def first_sends():
        made = []
        for k in range(1, 4):
            made.append(send_block(posx, own_slot, 0, at_x(k), k - 1))
        for k, step in enumerate((1, -1, far)):
            made.append(send_block(posx, own_slot, 1, at_z(step), 3 + k))
        for k, step in enumerate((1, -1, far)):
            made.append(send_block(posx, own_slot, 0, at_z(step), 6 + k))
        for k in range(1, 4):
            made.append(send_block(posx, own_slot, 1, at_x(k), 9 + k - 1))
        return made

    @pl.when(mine)
    def _():
        for copy in first_sends():
            copy.start()
        own_copy().start()

    lat_slot = lax.rem(sq, 8)

    def lat_target(n):
        return base + sq // 8, 8 * c + n

    def lat_copy(n):
        return pltpu.make_async_remote_copy(
            src_ref=latx.at[n // 2], dst_ref=lat.at[lat_slot], send_sem=lat_send.at[n],
            recv_sem=lat_recv.at[lat_slot], device_id=lat_target(n), device_id_type=MESH)

    def lat_local(n):
        return pltpu.make_async_copy(latx.at[n // 2], lat.at[lat_slot], lat_recv.at[lat_slot])

    for n in range(8):
        to_q, to_s = lat_target(n)
        away = jnp.logical_or(to_q != qd, to_s != sq)

        @pl.when(away)
        def _(n=n):
            lat_copy(n).start()

        @pl.when(jnp.logical_not(away))
        def _(n=n):
            lat_local(n).start()

    for j in range(3):
        e3[C * j : C * j + C, :] = ew[...]

    def turn(src, dst, first, count):
        def one(i, carry):
            o = pl.multiple_of(i * 128, 128)
            dst[pl.ds(o, 128), :] = src[:, pl.ds(o, 128)].T
            return carry

        lax.fori_loop(first, first + count, one, 0)

    weights(1).wait()
    turn(wqkv, wt, 9, 9)
    weights(2).wait()
    turn(wqkv, wt, 18, 9)

    def row_relays(k):
        src = lax.rem(xx + k, 4)
        slot = rz * 4 + src
        step = 2 - 4 * lax.rem(src, 2)
        return [
            send_block(pos.at[slot], slot, 0, at_z(s), 12 + 3 * (k - 1) + n)
            for n, s in enumerate((1, -1, step))
        ]

    def column_relays(r):
        slot = r * 4 + xx
        return [send_block(pos.at[slot], slot, 1, at_x(k), 21 + 3 * r + k - 1) for k in range(1, 4)]

    @pl.when(mine)
    def _():
        for k in range(1, 4):
            block_wait(rz * 4 + lax.rem(xx + k, 4), 0)
            for copy in row_relays(k):
                copy.start()

    for r in range(2):

        @pl.when(jnp.logical_not(jnp.logical_and(mine, rz == r)))
        def _(r=r):
            block_wait(r * 4 + xx, 1)
            for copy in column_relays(r):
                copy.start()

    weights(0).wait()
    turn(wqkv, wt, 0, 9)
    weights(3).wait()
    turn(wo, wot, 0, 9)

    for n in range(8):
        pltpu.make_async_copy(lat.at[n], lat.at[n], lat_recv.at[n]).wait()

    stepf = lat[0, 16:17, 0:1]
    acc = jnp.zeros((5, D), F32)
    for i in range(mod.shape[0]):
        acc = acc + jnp.where(stepf == float(i), mod[i], 0.0)
    mods[0:5, :] = acc
    mods[5:8, :] = jnp.zeros((3, D), F32)
    modsT[...] = mods[...].T
    lane = lax.broadcasted_iota(jnp.int32, levels.shape, 1).astype(F32)
    low = jnp.sum(jnp.where(lane == stepf, levels[...], 0.0), axis=1, keepdims=True)
    high = jnp.sum(jnp.where(lane == stepf + 1.0, levels[...], 0.0), axis=1, keepdims=True)
    step_size = high - low

    @pl.when(mine)
    def _():
        own_copy().wait()

    ones = (lax.broadcasted_iota(jnp.int32, (HP - HD, 256), 0) == 0).astype(F32)
    nothing = jnp.zeros((HP - HD, 256), F32)
    heads_at_once = 4
    rows_at_once = heads_at_once * HD

    def kv_copy(pair, which):
        ref = (kT, vT)[which]
        cols = pl.ds(pl.multiple_of(c * 1024 + pair * 256, 256), 256)
        return pltpu.make_async_remote_copy(
            src_ref=ref.at[:, :, cols], dst_ref=ref.at[:, :, cols], send_sem=kv_send.at[pair, which],
            recv_sem=kv_recv.at[pair, which], device_id=partner, device_id_type=MESH)

    def kv_wait(pair, which):
        ref = (kT, vT)[which]
        cols = pl.ds(pl.multiple_of((1 - c) * 1024 + pair * 256, 256), 256)
        dst = ref.at[:, :, cols]
        pltpu.make_async_copy(dst, dst, kv_recv.at[pair, which]).wait()

    def one_pair(n, carry):
        row = lax.rem(rz + n // 2, 2)
        pair = row * 2 + lax.rem(n, 2)
        for k in range(2):
            slot = pair * 2 + k
            column = lax.rem(slot, 4)

            @pl.when(jnp.logical_not(jnp.logical_and(mine, row == rz)))
            def _(slot=slot):
                block_wait(slot, 0)

            @pl.when(column != xx)
            def _(slot=slot):
                block_wait(slot, 1)

        a, b = pair * 2, pair * 2 + 1
        l3 = jnp.concatenate([split3(lat[a, 0:C]), split3(lat[b, 0:C])], axis=1)
        places = jnp.concatenate([pos[a, 0:TXT], pos[b, 0:TXT]], axis=0)
        hidden = tn(l3, e3[...]) + places.astype(F32)
        center = hidden - jnp.mean(hidden, axis=-1, keepdims=True)
        unit = center * lax.rsqrt(jnp.mean(center * center, axis=-1, keepdims=True) + EPS)
        xb = (unit * (1.0 + mods[1:2]) + mods[0:1]).astype(BF)
        x[pair] = xb
        cols = pl.ds(pl.multiple_of(c * 1024 + pair * 256, 256), 256)
        for g in range(H // heads_at_once):
            o = D + g * rows_at_once
            r = nt(wt[o : o + rows_at_once, :], xb)
            for j in range(heads_at_once):
                rows = r[j * HD : (j + 1) * HD].astype(BF).astype(F32)
                padded = jnp.concatenate([head_norm(rows, gains[1]), nothing], axis=0)
                kT[g * heads_at_once + j, :, cols] = padded.astype(BF)
        for g in range(H // heads_at_once):
            o = 2 * D + g * rows_at_once
            r = nt(wt[o : o + rows_at_once, :], xb)
            for j in range(heads_at_once):
                padded = jnp.concatenate([r[j * HD : (j + 1) * HD], ones], axis=0)
                vT[g * heads_at_once + j, :, cols] = padded.astype(BF)
        for k in range(2):
            slot = pair * 2 + k
            t = jnp.concatenate([pos[slot, TXT:ROWS, 128 * j : 128 * j + 128] for j in range(9)], axis=0)
            t = t.astype(F32)
            keys = jnp.concatenate([head_norm(t[0:HD], gains[1, :, 0:128]), nothing[:, 0:128]], axis=0)
            tk[8 * c + slot] = keys.astype(BF)
            tv[8 * c + slot] = jnp.concatenate([t[HD : 2 * HD], ones[:, 0:128]], axis=0).astype(BF)

        @pl.when(n > 0)
        def _():
            before = lax.rem(rz + (n - 1) // 2, 2) * 2 + lax.rem(n - 1, 2)
            kv_copy(before, 0).start()
            kv_copy(before, 1).start()

        return carry

    lax.fori_loop(0, 4, one_pair, 0)

    def one_query_block(n, carry):
        xb = x[part * 2 + n]
        cols = pl.ds(pl.multiple_of(n * 256, 256), 256)
        for g in range(H // heads_at_once):
            o = g * rows_at_once
            r = nt(wt[o : o + rows_at_once, :], xb)
            for j in range(heads_at_once):
                rows = r[j * HD : (j + 1) * HD].astype(BF).astype(F32)
                padded = jnp.concatenate([head_norm(rows, gains[0]), jnp.zeros((128 - HD, 256), F32)], axis=0)
                q[g * heads_at_once + j, cols, :] = padded.T.astype(BF)

        @pl.when(n == 0)
        def _():
            last = lax.rem(rz + 1, 2) * 2 + 1
            kv_copy(last, 0).start()
            kv_copy(last, 1).start()
            for which in range(2):
                tx_copy(which).start()

        return carry

    def tx_copy(which):
        ref = (tk, tv)[which]
        rows = pl.ds(8 * c, 8)
        return pltpu.make_async_remote_copy(
            src_ref=ref.at[rows], dst_ref=ref.at[rows], send_sem=tx_send.at[which],
            recv_sem=tx_recv.at[which], device_id=partner, device_id_type=MESH)

    def tx_wait(which):
        dst = (tk, tv)[which].at[pl.ds(8 * (1 - c), 8)]
        pltpu.make_async_copy(dst, dst, tx_recv.at[which]).wait()

    lax.fori_loop(0, 2, one_query_block, 0)
    for which in range(2):
        tx_wait(which)
        for pair in range(4):
            kv_wait(pair, which)

    def one_head(n, carry):
        made = []
        for half in range(2):
            qh = q[n, half * 256 : half * 256 + 256, 0:HP]
            p = jnp.exp2(nn(qh, kT[n])).astype(BF)
            own = nt(vT[n], p)
            pt = jnp.exp2(nn(qh, tk[n])).astype(BF)
            text = nt(tv[n], pt)
            made.append(own[0:HD] / own[HD : HD + 1] + text[0:HD] / text[HD : HD + 1])
        att[pl.ds(pl.multiple_of(n * HD, 8), HD), :] = jnp.concatenate(made, axis=1)
        return carry

    lax.fori_loop(0, H, one_head, 0)

    attb[...] = att[...].astype(BF)
    for t in range(4):
        slot = part * 4 + t
        hid[:, t * 128 : t * 128 + 128] = tn(e3[...], split3(lat[slot, 0:C])) + pos[slot, 0:TXT].T.astype(F32)
    for g in range(2):
        r = slice(g * 576, g * 576 + 576)
        hid[r, :] = hid[r, :] + modsT[r, 2:3] * nn(wot[r, :], attb[...])
    hidden = hid[...]
    center = hidden - jnp.sum(hidden, axis=0, keepdims=True) * (1.0 / D)
    scale = lax.rsqrt(jnp.sum(center * center, axis=0, keepdims=True) * (1.0 / D) + EPS)
    xb = (center * scale * (1.0 + modsT[:, 4:5]) + modsT[:, 3:4]).astype(BF)
    speed = tn(fw[...], xb)
    for t in range(4):
        piece = speed[:, t * 128 : t * 128 + 128]
        vbuf[t] = piece
        ubuf[t] = lat[part * 4 + t, 0:C] + step_size * piece

    whole = (qd // 2) * 8 + frame
    before = jnp.maximum(whole - 1, 0)

    def out_copy(which, t):
        src, dst, place = ((vbuf, vel, whole), (ubuf, adv, before))[which]
        there = lax.rem(place, 4)
        return pltpu.make_async_remote_copy(
            src_ref=src.at[t], dst_ref=dst.at[there], send_sem=out_send.at[which, t],
            recv_sem=out_recv.at[which, there],
            device_id=(place // 4, 8 * c + 4 * part + t), device_id_type=MESH)

    def out_local(which, t):
        src, dst, place = ((vbuf, vel, whole), (ubuf, adv, before))[which]
        there = lax.rem(place, 4)
        return pltpu.make_async_copy(src.at[t], dst.at[there], out_recv.at[which, there])

    def out_cases(which, t):
        place = (whole, before)[which]
        here = jnp.logical_and(place // 4 == qd, 8 * c + 4 * part + t == sq)
        away = jnp.logical_not(here)
        if which == 1:
            here = jnp.logical_and(here, whole > 0)
            away = jnp.logical_and(away, whole > 0)
        return here, away

    for which in range(2):
        for t in range(4):
            here, away = out_cases(which, t)

            @pl.when(away)
            def _(which=which, t=t):
                out_copy(which, t).start()

            @pl.when(here)
            def _(which=which, t=t):
                out_local(which, t).start()

    @pl.when(mine)
    def _():
        for copy in first_sends():
            copy.wait_send()
        for k in range(1, 4):
            for copy in row_relays(k):
                copy.wait_send()

    for r in range(2):

        @pl.when(jnp.logical_not(jnp.logical_and(mine, rz == r)))
        def _(r=r):
            for copy in column_relays(r):
                copy.wait_send()

    for n in range(8):
        to_q, to_s = lat_target(n)

        @pl.when(jnp.logical_or(to_q != qd, to_s != sq))
        def _(n=n):
            lat_copy(n).wait_send()

    for which in range(2):
        tx_copy(which).wait_send()
        for pair in range(4):
            kv_copy(pair, which).wait_send()
        for t in range(4):

            @pl.when(out_cases(which, t)[1])
            def _(which=which, t=t):
                out_copy(which, t).wait_send()

    for n in range(4):
        pltpu.make_async_copy(vel.at[n], vel.at[n], out_recv.at[0, n]).wait()
    for n in range(3):
        pltpu.make_async_copy(adv.at[n], adv.at[n], out_recv.at[1, n]).wait()

    @pl.when(qd < 15)
    def _():
        pltpu.make_async_copy(adv.at[3], adv.at[3], out_recv.at[1, 3]).wait()

    @pl.when(qd == 15)
    def _():
        adv[3] = noise[...]


def body(
    latents, step_index, levels, modulation, embed_weight, position, qkv_weight, q_gain, k_gain,
    text_kv, out_weight, final_weight, new_noise,
):
    frames = latents.shape[0]
    steps = jnp.broadcast_to(step_index.astype(F32)[:, None, None], (frames, 8, 128))
    latx = jnp.concatenate([latents, steps], axis=1)
    text = jnp.swapaxes(text_kv, 1, 2).reshape(9, 16, TXT)
    posx = jnp.concatenate([position, jnp.swapaxes(text, 0, 1).reshape(16, D)], axis=0)
    fold = math.log2(math.e) / math.sqrt(HD)
    gains = jnp.broadcast_to(jnp.stack([q_gain * fold, k_gain])[:, :, None], (2, HD, 256))
    inner = pl.BlockSpec(memory_space=pltpu.VMEM)
    outer = pl.BlockSpec(memory_space=pl.ANY)
    dma = pltpu.SemaphoreType.DMA
    return pl.pallas_call(
        kernel,
        out_shape=(jax.ShapeDtypeStruct(latents.shape, F32),) * 2,
        in_specs=[inner] * 8 + [outer] * 2,
        out_specs=(inner, inner),
        scratch_shapes=[
            pltpu.VMEM((8, ROWS, D), BF),
            pltpu.VMEM((8, 24, 128), F32),
            pltpu.VMEM((D, 3 * D), BF),
            pltpu.VMEM((D, D), BF),
            pltpu.VMEM((3 * D, D), BF),
            pltpu.VMEM((D, D), BF),
            pltpu.VMEM((3 * C, D), BF),
            pltpu.VMEM((8, D), F32),
            pltpu.VMEM((D, 8), F32),
            pltpu.VMEM((4, 256, D), BF),
            pltpu.VMEM((H, HP, 2048), BF),
            pltpu.VMEM((H, HP, 2048), BF),
            pltpu.VMEM((H, 512, 128), BF),
            pltpu.VMEM((H, HP, TXT), BF),
            pltpu.VMEM((H, HP, TXT), BF),
            pltpu.VMEM((D, 512), F32),
            pltpu.VMEM((D, 512), BF),
            pltpu.VMEM((D, 512), F32),
            pltpu.VMEM((4, C, 128), F32),
            pltpu.VMEM((4, C, 128), F32),
            dma((4,)),
            dma((1,)),
            dma((27,)),
            dma((8, 2)),
            dma((8,)),
            dma((8,)),
            dma((4, 2)),
            dma((4, 2)),
            dma((2,)),
            dma((2,)),
            dma((2, 4)),
            dma((2, 4)),
        ],
        compiler_params=pltpu.CompilerParams(
            vmem_limit_bytes=62 * 1024 * 1024, has_side_effects=True
        ),
        name="denoise",
    )(
        latx, posx, modulation, levels[None, :], gains, embed_weight, final_weight, new_noise,
        qkv_weight, out_weight,
    )


def solution(mesh):
    in_specs = (
        P("queue", None, "seq"), P("queue"), P(), P(), P(), P("seq", None), P(), P(), P(),
        P(None, None, "seq"), P(), P(), P(None, "seq"),
    )
    out_specs = (P("queue", None, "seq"), P("queue", None, "seq"))
    return jax.shard_map(body, mesh=mesh, in_specs=in_specs, out_specs=out_specs, check_vma=False)
```

time: 273 us -> 101 us (0.37)
  the two profiles are of different devices: /device:TPU:89 before, /device:TPU:8 now
where the time goes in v1:
time: 101 us; the launch traced here: 100 us
  Pallas kernels  86.1 us (85%)
  local copies, waits for them, and re-layouts  8.54 us (8%)
  other arithmetic  5.08 us (5%)
    pallas_call x1, Pallas kernels, body(): pl.pallas_call(kernel, out_shape=(jax.ShapeDtypeStruct(latents.shape, F32...  86.1 us
    unnamed x5, local copies, waits for them, and re-layouts  6.94 us

profile of v1, /device:TPU:8, one launch (start us, length us, event | category | flops | bytes accessed | tf_op | source)
XLA Modules:
  0.0 100.4 jit_solution(15219703689149886294)
XLA Ops:
  0.6 0.7 convert_element_type.3
  1.3 0.7 multiply_bitcast_fusion
  1.9 0.7 pad_maximum_fusion.2
  2.6 0.1 broadcast_in_dim.6
  2.7 1.4 %pad_maximum_fusion.1.latx = f32[4,24,128]{2,1,0:T(8,128)} fusion(f32[4,8,128]{2,1,0:T(8,128)S(1)} %broadcast_in_dim.6, f32[4,16,128]{2,1,0:T(8,128)} %param.13), kind=kLoop, calls=%fused_computation.1 | loop fusion | flops 12288 | bytes 98304 | tf_op jit(solution)/shard_map/concatenate | solution.py:447
  4.1 0.8 copy.18
  4.9 0.7 broadcast_in_dim.8.gains
  5.6 1.7 %pad_maximum_fusion.posx = bf16[144,1152]{1,0:T(8,128)(2,1)} fusion(bf16[16,1152]{1,0:T(8,128)(2,1)S(1)} %bitcast.13, bf16[128,1152]{1,0:T(8,128)(2,1)} %param.18), kind=kLoop, calls=%fused_computation | loop fusion | flops 663552 | bytes 663552 | tf_op jit(solution)/shard_map/concatenate | solution.py:449
  7.3 1.7 %copy.20.fw = bf16[1152,16]{1,0:T(8,128)(2,1)} copy(bf16[1152,16]{0,1:T(8,128)(2,1)} %param.24) | data formatting | bytes 73728 | tf_op args[11]
  9.0 2.5 %copy.19.mod = f32[30,5,1152]{2,1,0:T(8,128)} copy(f32[30,5,1152]{2,0,1:T(8,128)} %param.16) | data formatting | bytes 1382400 | tf_op args[3]
  11.5 86.1 %denoise.1 = (f32[4,16,128]{2,1,0:T(8,128)}, f32[4,16,128]{2,1,0:T(8,128)}) custom-call(f32[4,24,128]{2,1,0:T(8,128)} %pad_maximum_fusion.1.latx, bf16[144,1152]{1,0:T(8,128)(2,1)} %pad_maximum_fusion.posx, f32[30,5,1152]{2,1,0:T(8,128)} %copy.19.mod, f32[1,31]{1,0:T(1,128)} %bitcast.15, f32[2,72,256]{2,1,0:T(8,128)} %broadcast_in_dim.8.gains, ...), custom_call_target="tpu_custom_call" | custom-call | tf_op jit(solution)/shard_map/denoise/pallas_call | solution.py:455
  97.6 1.4 %copy.26 = f32[4,16,128]{2,1,0:T(8,128)} copy(f32[4,16,128]{2,1,0:T(8,128)} %get-tuple-element.4) | data formatting | bytes 65536
  99.0 1.4 %copy.27 = f32[4,16,128]{2,1,0:T(8,128)} copy(f32[4,16,128]{2,1,0:T(8,128)} %get-tuple-element.5) | data formatting | bytes 65536
  (1 shorter events, 0.0 us)

commit v2 on v1

--- a/solution.py
+++ b/solution.py
@@ -43,9 +43,9 @@
 
 
 def kernel(
-    latx, posx, mod, levels, gains, ew, fw, noise, wqkv_hbm, wo_hbm,
-    adv, vel,
-    pos, lat, wqkv, wo, wt, wot, e3, mods, modsT, x, kT, vT, q, tk, tv, att, attb, hid, ubuf, vbuf,
+    latents, steps, posin, text, mod, levels, qg, kg, ew, fw, noise, wqkv_hbm, wo_hbm,
+    out,
+    pos, lat, latx, gains8, gains, wqkv, wo, wt, wot, e3, mods, modsT, x, kT, vT, q, tk, tv, att, attb, hid, ubuf, vbuf,
     w_sem, own_sem, pos_send, pos_recv, lat_send, lat_recv, kv_send, kv_recv, tx_send, tx_recv,
     out_send, out_recv,
 ):
@@ -66,7 +66,7 @@
         return ((zz // 4) * 8 + y * 2 + c, lax.rem(zz, 4) * 4 + xx)
 
     def at_x(step):
-        return (qd, zl * 4 + lax.rem(xx + step, 4))
+        return (qd, zl * 4 + lax.rem(xx + step + 4, 4))
 
     def weights(k):
         if k < 3:
@@ -76,6 +76,28 @@
 
     for k in range(4):
         weights(k).start()
+
+    barrier = pltpu.get_barrier_semaphore()
+
+    def greet(target):
+        pl.semaphore_signal(barrier, inc=1, device_id=target, device_id_type=MESH)
+
+    for target in (at_x(1), at_x(-1), at_z(1), at_z(-1), partner):
+        greet(target)
+    for n in range(8):
+
+        @pl.when(jnp.logical_or(base + h != qd, 8 * c + n != sq))
+        def _(n=n):
+            greet((base + h, 8 * c + n))
+
+    after = (qd + 1) // 2 * 2
+
+    @pl.when(qd < 15)
+    def _():
+        greet((after + h, 8 * lax.rem(qd + 1, 2) + lax.rem(sq, 8) // 4))
+
+    starts = jnp.logical_or(sq // 2 == 4, jnp.logical_and(sq // 2 == 0, base > 0))
+    pl.semaphore_wait(barrier, 13 - jnp.where(c == h, 1, 0) + jnp.where(starts, 4, 0))
 
     def rows_of(ref, color):
         low, size = PARTS[color]
@@ -97,28 +119,82 @@
 
     own_slot = rz * 4 + xx
     mine = c == h
-    far = 2 - 4 * lax.rem(xx, 2)
-
-    def own_copy():
-        return pltpu.make_async_copy(posx, pos.at[own_slot], own_sem.at[0])
-
-    def first_sends():
-        made = []
-        for k in range(1, 4):
-            made.append(send_block(posx, own_slot, 0, at_x(k), k - 1))
-        for k, step in enumerate((1, -1, far)):
-            made.append(send_block(posx, own_slot, 1, at_z(step), 3 + k))
-        for k, step in enumerate((1, -1, far)):
-            made.append(send_block(posx, own_slot, 0, at_z(step), 6 + k))
-        for k in range(1, 4):
-            made.append(send_block(posx, own_slot, 1, at_x(k), 9 + k - 1))
+    odd = lax.rem(xx, 2)
+
+    def own_copies():
+        made = [pltpu.make_async_copy(posin, pos.at[own_slot, pl.ds(0, TXT), :], own_sem.at[9])]
+        for j in range(9):
+            dst = pos.at[own_slot, pl.ds(TXT, 16), pl.ds(128 * j, 128)]
+            made.append(pltpu.make_async_copy(text.at[j], dst, own_sem.at[j]))
         return made
 
+    def first_sends(color):
+        src = posin if color == 0 else pos.at[own_slot]
+        targets = (at_x(1), at_x(-1), at_z(1), at_z(-1))
+        return [send_block(src, own_slot, color, t, 4 * color + k) for k, t in enumerate(targets)]
+
+    def row_relays(k):
+        slot = rz * 4 + lax.rem(xx + k, 4)
+        return [send_block(pos.at[slot], slot, 0, at_z(s), 8 + 2 * (k - 1) + n) for n, s in enumerate((1, -1))]
+
+    def row_hop():
+        step = 2 * odd - 1
+        slot = rz * 4 + lax.rem(xx - step + 4, 4)
+        return send_block(pos.at[slot], slot, 0, at_x(step), 14)
+
+    def column_relays(r):
+        slot = r * 4 + xx
+        return [send_block(pos.at[slot], slot, 1, at_x(s), 15 + 2 * r + n) for n, s in enumerate((1, -1))]
+
+    def delta(row):
+        return lax.rem(2 * c + row - zl + 4, 4)
+
+    def near(row):
+        return lax.rem(delta(row), 2) == 1
+
+    def z_hop(slot, color, row, number):
+        return send_block(pos.at[slot], slot, color, at_z(delta(row) - 2), number)
+
+    def column_hop_due(r):
+        return jnp.logical_and(near(r), odd == jnp.where(delta(r) == 3, 0, 1))
+
+    def row_hop_slot(r, k):
+        return r * 4 + 2 * k + jnp.where(delta(r) == 3, 0, 1)
+
+    def across_slot(r):
+        return r * 4 + lax.rem(xx + (3, 1)[r], 4)
+
+    def across_slot_of(row):
+        return row * 4 + lax.rem(xx + 3 - 2 * row, 4)
+
+    def across_hop(r):
+        slot = across_slot(r)
+        return send_block(pos.at[slot], slot, 1, at_x((1, -1)[r]), 25 + r)
+
     @pl.when(mine)
     def _():
-        for copy in first_sends():
+        for copy in first_sends(0):
             copy.start()
-        own_copy().start()
+        for copy in own_copies():
+            copy.start()
+
+    for n in range(4):
+        latx[n, 0:C] = latents[n]
+        latx[n, C:24] = jnp.full((8, 128), steps[n].astype(F32))
+    fold = math.log2(math.e) / math.sqrt(HD)
+    gains8[...] = jnp.zeros((8, 128), F32)
+    gains8[0:1, 0:HD] = qg[...] * fold
+    gains8[1:2, 0:HD] = kg[...]
+    columns = gains8[...].T
+    for k in range(2):
+        gains[k] = jnp.broadcast_to(columns[0:HD, k : k + 1], (HD, 256))
+
+    @pl.when(mine)
+    def _():
+        for copy in own_copies():
+            copy.wait()
+        for copy in first_sends(1):
+            copy.start()
 
     lat_slot = lax.rem(sq, 8)
 
@@ -158,32 +234,43 @@
 
     weights(1).wait()
     turn(wqkv, wt, 9, 9)
+
+    @pl.when(mine)
+    def _():
+        for k in (1, 3):
+            block_wait(rz * 4 + lax.rem(xx + k, 4), 0)
+        row_hop().start()
+        for k in (1, 3):
+            for copy in row_relays(k):
+                copy.start()
+
+    for r in range(2):
+
+        @pl.when(near(r))
+        def _(r=r):
+            block_wait(r * 4 + xx, 1)
+
+        @pl.when(column_hop_due(r))
+        def _(r=r):
+            z_hop(r * 4 + xx, 1, r, 19 + r).start()
+
+        @pl.when(near(r))
+        def _(r=r):
+            for copy in column_relays(r):
+                copy.start()
+
     weights(2).wait()
     turn(wqkv, wt, 18, 9)
 
-    def row_relays(k):
-        src = lax.rem(xx + k, 4)
-        slot = rz * 4 + src
-        step = 2 - 4 * lax.rem(src, 2)
-        return [
-            send_block(pos.at[slot], slot, 0, at_z(s), 12 + 3 * (k - 1) + n)
-            for n, s in enumerate((1, -1, step))
-        ]
-
-    def column_relays(r):
-        slot = r * 4 + xx
-        return [send_block(pos.at[slot], slot, 1, at_x(k), 21 + 3 * r + k - 1) for k in range(1, 4)]
-
     @pl.when(mine)
     def _():
-        for k in range(1, 4):
-            block_wait(rz * 4 + lax.rem(xx + k, 4), 0)
-            for copy in row_relays(k):
-                copy.start()
+        block_wait(rz * 4 + lax.rem(xx + 2, 4), 0)
+        for copy in row_relays(2):
+            copy.start()
 
     for r in range(2):
 
-        @pl.when(jnp.logical_not(jnp.logical_and(mine, rz == r)))
+        @pl.when(delta(r) == 2)
         def _(r=r):
             block_wait(r * 4 + xx, 1)
             for copy in column_relays(r):
@@ -191,6 +278,19 @@
 
     weights(0).wait()
     turn(wqkv, wt, 0, 9)
+
+    for r in range(2):
+
+        @pl.when(near(r))
+        def _(r=r):
+            for k in range(2):
+                block_wait(row_hop_slot(r, k), 0)
+                z_hop(row_hop_slot(r, k), 0, r, 21 + 2 * r + k).start()
+
+    for r in range(2):
+        block_wait(across_slot(r), 1)
+        across_hop(r).start()
+
     weights(3).wait()
     turn(wo, wot, 0, 9)
 
@@ -198,10 +298,9 @@
         pltpu.make_async_copy(lat.at[n], lat.at[n], lat_recv.at[n]).wait()
 
     stepf = lat[0, 16:17, 0:1]
-    acc = jnp.zeros((5, D), F32)
-    for i in range(mod.shape[0]):
-        acc = acc + jnp.where(stepf == float(i), mod[i], 0.0)
-    mods[0:5, :] = acc
+    plan = lax.broadcasted_iota(jnp.int32, mod.shape[1:], 0).astype(F32)
+    for i in range(5):
+        mods[i : i + 1, :] = jnp.sum(jnp.where(plan == stepf, mod[i], 0.0), axis=0, keepdims=True)
     mods[5:8, :] = jnp.zeros((3, D), F32)
     modsT[...] = mods[...].T
     lane = lax.broadcasted_iota(jnp.int32, levels.shape, 1).astype(F32)
@@ -209,10 +308,6 @@
     high = jnp.sum(jnp.where(lane == stepf + 1.0, levels[...], 0.0), axis=1, keepdims=True)
     step_size = high - low
 
-    @pl.when(mine)
-    def _():
-        own_copy().wait()
-
     ones = (lax.broadcasted_iota(jnp.int32, (HP - HD, 256), 0) == 0).astype(F32)
     nothing = jnp.zeros((HP - HD, 256), F32)
     heads_at_once = 4
@@ -231,18 +326,23 @@
         dst = ref.at[:, :, cols]
         pltpu.make_async_copy(dst, dst, kv_recv.at[pair, which]).wait()
 
+    def nth_row(n):
+        return lax.rem(jnp.where(mine, rz, 1 - rz) + n // 2, 2)
+
     def one_pair(n, carry):
-        row = lax.rem(rz + n // 2, 2)
+        row = nth_row(n)
         pair = row * 2 + lax.rem(n, 2)
         for k in range(2):
             slot = pair * 2 + k
             column = lax.rem(slot, 4)
 
-            @pl.when(jnp.logical_not(jnp.logical_and(mine, row == rz)))
+            passed = jnp.where(delta(row) == 3, 0, jnp.where(delta(row) == 1, 1, 2))
+
+            @pl.when(jnp.logical_and(delta(row) > 0, lax.rem(slot, 2) != passed))
             def _(slot=slot):
                 block_wait(slot, 0)
 
-            @pl.when(column != xx)
+            @pl.when(jnp.logical_and(column != xx, slot != across_slot_of(row)))
             def _(slot=slot):
                 block_wait(slot, 1)
 
@@ -278,7 +378,7 @@
 
         @pl.when(n > 0)
         def _():
-            before = lax.rem(rz + (n - 1) // 2, 2) * 2 + lax.rem(n - 1, 2)
+            before = nth_row(n - 1) * 2 + lax.rem(n - 1, 2)
             kv_copy(before, 0).start()
             kv_copy(before, 1).start()
 
@@ -299,7 +399,7 @@
 
         @pl.when(n == 0)
         def _():
-            last = lax.rem(rz + 1, 2) * 2 + 1
+            last = nth_row(3) * 2 + 1
             kv_copy(last, 0).start()
             kv_copy(last, 1).start()
             for which in range(2):
@@ -349,7 +449,7 @@
     center = hidden - jnp.sum(hidden, axis=0, keepdims=True) * (1.0 / D)
     scale = lax.rsqrt(jnp.sum(center * center, axis=0, keepdims=True) * (1.0 / D) + EPS)
     xb = (center * scale * (1.0 + modsT[:, 4:5]) + modsT[:, 3:4]).astype(BF)
-    speed = tn(fw[...], xb)
+    speed = nn(fw[...], xb)
     for t in range(4):
         piece = speed[:, t * 128 : t * 128 + 128]
         vbuf[t] = piece
@@ -359,17 +459,17 @@
     before = jnp.maximum(whole - 1, 0)
 
     def out_copy(which, t):
-        src, dst, place = ((vbuf, vel, whole), (ubuf, adv, before))[which]
+        src, dst, place = ((vbuf, 0, whole), (ubuf, 1, before))[which]
         there = lax.rem(place, 4)
         return pltpu.make_async_remote_copy(
-            src_ref=src.at[t], dst_ref=dst.at[there], send_sem=out_send.at[which, t],
+            src_ref=src.at[t], dst_ref=out.at[dst, there], send_sem=out_send.at[which, t],
             recv_sem=out_recv.at[which, there],
             device_id=(place // 4, 8 * c + 4 * part + t), device_id_type=MESH)
 
     def out_local(which, t):
-        src, dst, place = ((vbuf, vel, whole), (ubuf, adv, before))[which]
+        src, dst, place = ((vbuf, 0, whole), (ubuf, 1, before))[which]
         there = lax.rem(place, 4)
-        return pltpu.make_async_copy(src.at[t], dst.at[there], out_recv.at[which, there])
+        return pltpu.make_async_copy(src.at[t], out.at[dst, there], out_recv.at[which, there])
 
     def out_cases(which, t):
         place = (whole, before)[which]
@@ -394,18 +494,31 @@
 
     @pl.when(mine)
     def _():
-        for copy in first_sends():
-            copy.wait_send()
+        for color in range(2):
+            for copy in first_sends(color):
+                copy.wait_send()
+        row_hop().wait_send()
         for k in range(1, 4):
             for copy in row_relays(k):
                 copy.wait_send()
 
     for r in range(2):
 
-        @pl.when(jnp.logical_not(jnp.logical_and(mine, rz == r)))
+        @pl.when(delta(r) > 0)
         def _(r=r):
             for copy in column_relays(r):
                 copy.wait_send()
+
+        @pl.when(column_hop_due(r))
+        def _(r=r):
+            z_hop(r * 4 + xx, 1, r, 19 + r).wait_send()
+
+        @pl.when(near(r))
+        def _(r=r):
+            for k in range(2):
+                z_hop(row_hop_slot(r, k), 0, r, 21 + 2 * r + k).wait_send()
+
+        across_hop(r).wait_send()
 
     for n in range(8):
         to_q, to_s = lat_target(n)
@@ -424,42 +537,41 @@
             def _(which=which, t=t):
                 out_copy(which, t).wait_send()
 
-    for n in range(4):
-        pltpu.make_async_copy(vel.at[n], vel.at[n], out_recv.at[0, n]).wait()
-    for n in range(3):
-        pltpu.make_async_copy(adv.at[n], adv.at[n], out_recv.at[1, n]).wait()
+    for which, count in ((0, 4), (1, 3)):
+        for n in range(count):
+            dst = out.at[which, n]
+            pltpu.make_async_copy(dst, dst, out_recv.at[which, n]).wait()
 
     @pl.when(qd < 15)
     def _():
-        pltpu.make_async_copy(adv.at[3], adv.at[3], out_recv.at[1, 3]).wait()
+        dst = out.at[1, 3]
+        pltpu.make_async_copy(dst, dst, out_recv.at[1, 3]).wait()
 
     @pl.when(qd == 15)
     def _():
-        adv[3] = noise[...]
+        out[1, 3] = noise[...]
 
 
 def body(
     latents, step_index, levels, modulation, embed_weight, position, qkv_weight, q_gain, k_gain,
     text_kv, out_weight, final_weight, new_noise,
 ):
-    frames = latents.shape[0]
-    steps = jnp.broadcast_to(step_index.astype(F32)[:, None, None], (frames, 8, 128))
-    latx = jnp.concatenate([latents, steps], axis=1)
     text = jnp.swapaxes(text_kv, 1, 2).reshape(9, 16, TXT)
-    posx = jnp.concatenate([position, jnp.swapaxes(text, 0, 1).reshape(16, D)], axis=0)
-    fold = math.log2(math.e) / math.sqrt(HD)
-    gains = jnp.broadcast_to(jnp.stack([q_gain * fold, k_gain])[:, :, None], (2, HD, 256))
     inner = pl.BlockSpec(memory_space=pltpu.VMEM)
     outer = pl.BlockSpec(memory_space=pl.ANY)
     dma = pltpu.SemaphoreType.DMA
-    return pl.pallas_call(
+    scalars = pl.BlockSpec(memory_space=pltpu.SMEM)
+    both = pl.pallas_call(
         kernel,
-        out_shape=(jax.ShapeDtypeStruct(latents.shape, F32),) * 2,
-        in_specs=[inner] * 8 + [outer] * 2,
-        out_specs=(inner, inner),
+        out_shape=jax.ShapeDtypeStruct((2,) + latents.shape, F32),
+        in_specs=[inner, scalars] + [inner] * 9 + [outer] * 2,
+        out_specs=inner,
         scratch_shapes=[
             pltpu.VMEM((8, ROWS, D), BF),
             pltpu.VMEM((8, 24, 128), F32),
+            pltpu.VMEM((4, 24, 128), F32),
+            pltpu.VMEM((8, 128), F32),
+            pltpu.VMEM((2, HD, 256), F32),
             pltpu.VMEM((D, 3 * D), BF),
             pltpu.VMEM((D, D), BF),
             pltpu.VMEM((3 * D, D), BF),
@@ -479,7 +591,7 @@
             pltpu.VMEM((4, C, 128), F32),
             pltpu.VMEM((4, C, 128), F32),
             dma((4,)),
-            dma((1,)),
+            dma((10,)),
             dma((27,)),
             dma((8, 2)),
             dma((8,)),
@@ -492,13 +604,14 @@
             dma((2, 4)),
         ],
         compiler_params=pltpu.CompilerParams(
-            vmem_limit_bytes=62 * 1024 * 1024, has_side_effects=True
+            vmem_limit_bytes=62 * 1024 * 1024, has_side_effects=True, collective_id=0
         ),
         name="denoise",
     )(
-        latx, posx, modulation, levels[None, :], gains, embed_weight, final_weight, new_noise,
-        qkv_weight, out_weight,
+        latents, step_index, position, text, jnp.swapaxes(modulation, 0, 1), levels[None, :],
+        q_gain[None, :], k_gain[None, :], embed_weight, final_weight.T, new_noise, qkv_weight, out_weight,
     )
+    return both[1], both[0]
 
 
 def solution(mesh):

time: 101 us -> 79.5 us (0.79)
  the two profiles are of different devices: /device:TPU:8 before, /device:TPU:49 now
where the time goes in v2:
time: 79.5 us; the launch traced here: 79 us
  Pallas kernels  77 us (97%)
  local copies, waits for them, and re-layouts  1.4 us (2%)
    pallas_call x1, Pallas kernels, body(): pl.pallas_call(kernel, out_shape=jax.ShapeDtypeStruct((2,) + latents.shap...  77 us

profile of v2, /device:TPU:49, one launch (start us, length us, event | category | flops | bytes accessed | tf_op | source)
XLA Modules:
  0.0 79.0 jit_solution(8324903944818069838)
XLA Ops:
  0.6 77.0 %denoise.1 = f32[2,4,16,128]{3,2,1,0:T(8,128)} custom-call(f32[4,16,128]{2,1,0:T(8,128)} %latents.1, s32[4]{0:T(128)} %steps.1, bf16[128,1152]{1,0:T(8,128)(2,1)} %posin.1, bf16[9,16,128]{2,1,0:T(8,128)(2,1)} %bitcast.13, f32[5,30,1152]{2,1,0:T(8,128)} %bitcast.12, f32[1,31]{1,0:T(1,128)} %bitcast.15, f32[1,72]{1,0:T(1,128)} %bitcast.16, f32[1,72]{1,0:T(1,128)} %bitcast.17, ...), custom_call_target="tpu_custom_call" | custom-call | tf_op jit(solution)/shard_map/denoise/pallas_call | solution.py:564
  77.6 1.4 %slice_bitcast_fusion = (f32[4,16,128]{2,1,0:T(8,128)}, f32[4,16,128]{2,1,0:T(8,128)}) fusion(f32[2,4,16,128]{3,2,1,0:T(8,128)} %denoise.1), kind=kLoop, calls=%fused_computation | loop fusion | bytes 131072 | tf_op jit(solution)/shard_map/squeeze | solution.py:614

commit v3 on v2

--- a/solution.py
+++ b/solution.py
@@ -45,7 +45,7 @@
 def kernel(
     latents, steps, posin, text, mod, levels, qg, kg, ew, fw, noise, wqkv_hbm, wo_hbm,
     out,
-    pos, lat, latx, gains8, gains, wqkv, wo, wt, wot, e3, mods, modsT, x, kT, vT, q, tk, tv, att, attb, hid, ubuf, vbuf,
+    pos, lat, latx, gains8, gains, wqkv, wo, wt, wot, e3, mods, modsT, x, kT, vT, q, p_even, p_odd, tk, tv, att, attb, hid, ubuf, vbuf,
     w_sem, own_sem, pos_send, pos_recv, lat_send, lat_recv, kv_send, kv_recv, tx_send, tx_recv,
     out_send, out_recv,
 ):
@@ -97,7 +97,8 @@
         greet((after + h, 8 * lax.rem(qd + 1, 2) + lax.rem(sq, 8) // 4))
 
     starts = jnp.logical_or(sq // 2 == 4, jnp.logical_and(sq // 2 == 0, base > 0))
-    pl.semaphore_wait(barrier, 13 - jnp.where(c == h, 1, 0) + jnp.where(starts, 4, 0))
+    with jax.named_scope("entry"):
+        pl.semaphore_wait(barrier, 13 - jnp.where(c == h, 1, 0) + jnp.where(starts, 4, 0))
 
     def rows_of(ref, color):
         low, size = PARTS[color]
@@ -232,8 +233,9 @@
 
         lax.fori_loop(first, first + count, one, 0)
 
-    weights(1).wait()
-    turn(wqkv, wt, 9, 9)
+    with jax.named_scope("turnk"):
+        weights(1).wait()
+        turn(wqkv, wt, 9, 9)
 
     @pl.when(mine)
     def _():
@@ -259,8 +261,9 @@
             for copy in column_relays(r):
                 copy.start()
 
-    weights(2).wait()
-    turn(wqkv, wt, 18, 9)
+    with jax.named_scope("turnv"):
+        weights(2).wait()
+        turn(wqkv, wt, 18, 9)
 
     @pl.when(mine)
     def _():
@@ -276,26 +279,9 @@
             for copy in column_relays(r):
                 copy.start()
 
-    weights(0).wait()
-    turn(wqkv, wt, 0, 9)
-
-    for r in range(2):
-
-        @pl.when(near(r))
-        def _(r=r):
-            for k in range(2):
-                block_wait(row_hop_slot(r, k), 0)
-                z_hop(row_hop_slot(r, k), 0, r, 21 + 2 * r + k).start()
-
-    for r in range(2):
-        block_wait(across_slot(r), 1)
-        across_hop(r).start()
-
-    weights(3).wait()
-    turn(wo, wot, 0, 9)
-
-    for n in range(8):
-        pltpu.make_async_copy(lat.at[n], lat.at[n], lat_recv.at[n]).wait()
+    with jax.named_scope("latents"):
+        for n in range(8):
+            pltpu.make_async_copy(lat.at[n], lat.at[n], lat_recv.at[n]).wait()
 
     stepf = lat[0, 16:17, 0:1]
     plan = lax.broadcasted_iota(jnp.int32, mod.shape[1:], 0).astype(F32)
@@ -329,20 +315,46 @@
     def nth_row(n):
         return lax.rem(jnp.where(mine, rz, 1 - rz) + n // 2, 2)
 
+    def nth_pair(n):
+        return nth_row(n) * 2 + lax.rem(xx // 2 + n, 2)
+
+    def later_hops():
+        first = nth_pair(0)
+        for r in range(2):
+
+            @pl.when(near(r))
+            def _(r=r):
+                for k in range(2):
+                    slot = row_hop_slot(r, k)
+
+                    @pl.when(slot // 2 != first)
+                    def _(slot=slot):
+                        block_wait(slot, 0)
+
+                    z_hop(slot, 0, r, 21 + 2 * r + k).start()
+
+        for r in range(2):
+
+            @pl.when(across_slot(r) // 2 != first)
+            def _(r=r):
+                block_wait(across_slot(r), 1)
+
+            across_hop(r).start()
+
     def one_pair(n, carry):
         row = nth_row(n)
-        pair = row * 2 + lax.rem(n, 2)
+        pair = nth_pair(n)
         for k in range(2):
             slot = pair * 2 + k
             column = lax.rem(slot, 4)
 
             passed = jnp.where(delta(row) == 3, 0, jnp.where(delta(row) == 1, 1, 2))
 
-            @pl.when(jnp.logical_and(delta(row) > 0, lax.rem(slot, 2) != passed))
+            @pl.when(jnp.logical_and(delta(row) > 0, jnp.logical_or(n == 0, lax.rem(slot, 2) != passed)))
             def _(slot=slot):
                 block_wait(slot, 0)
 
-            @pl.when(jnp.logical_and(column != xx, slot != across_slot_of(row)))
+            @pl.when(jnp.logical_and(column != xx, jnp.logical_or(n == 0, slot != across_slot_of(row))))
             def _(slot=slot):
                 block_wait(slot, 1)
 
@@ -368,6 +380,8 @@
             for j in range(heads_at_once):
                 padded = jnp.concatenate([r[j * HD : (j + 1) * HD], ones], axis=0)
                 vT[g * heads_at_once + j, :, cols] = padded.astype(BF)
+            if g == 0:
+                kv_copy(pair, 0).start()
         for k in range(2):
             slot = pair * 2 + k
             t = jnp.concatenate([pos[slot, TXT:ROWS, 128 * j : 128 * j + 128] for j in range(9)], axis=0)
@@ -376,15 +390,23 @@
             tk[8 * c + slot] = keys.astype(BF)
             tv[8 * c + slot] = jnp.concatenate([t[HD : 2 * HD], ones[:, 0:128]], axis=0).astype(BF)
 
-        @pl.when(n > 0)
+        kv_copy(pair, 1).start()
+
+        @pl.when(n == 0)
         def _():
-            before = nth_row(n - 1) * 2 + lax.rem(n - 1, 2)
-            kv_copy(before, 0).start()
-            kv_copy(before, 1).start()
+            later_hops()
+            weights(0).wait()
+            turn(wqkv, wt, 0, 9)
+
+        @pl.when(n == 1)
+        def _():
+            weights(3).wait()
+            turn(wo, wot, 0, 9)
 
         return carry
 
-    lax.fori_loop(0, 4, one_pair, 0)
+    with jax.named_scope("pairs"):
+        lax.fori_loop(0, 4, one_pair, 0)
 
     def one_query_block(n, carry):
         xb = x[part * 2 + n]
@@ -397,14 +419,6 @@
                 padded = jnp.concatenate([head_norm(rows, gains[0]), jnp.zeros((128 - HD, 256), F32)], axis=0)
                 q[g * heads_at_once + j, cols, :] = padded.T.astype(BF)
 
-        @pl.when(n == 0)
-        def _():
-            last = nth_row(3) * 2 + 1
-            kv_copy(last, 0).start()
-            kv_copy(last, 1).start()
-            for which in range(2):
-                tx_copy(which).start()
-
         return carry
 
     def tx_copy(which):
@@ -418,25 +432,50 @@
         dst = (tk, tv)[which].at[pl.ds(8 * (1 - c), 8)]
         pltpu.make_async_copy(dst, dst, tx_recv.at[which]).wait()
 
-    lax.fori_loop(0, 2, one_query_block, 0)
     for which in range(2):
-        tx_wait(which)
-        for pair in range(4):
-            kv_wait(pair, which)
-
-    def one_head(n, carry):
-        made = []
-        for half in range(2):
-            qh = q[n, half * 256 : half * 256 + 256, 0:HP]
-            p = jnp.exp2(nn(qh, kT[n])).astype(BF)
-            own = nt(vT[n], p)
-            pt = jnp.exp2(nn(qh, tk[n])).astype(BF)
-            text = nt(tv[n], pt)
-            made.append(own[0:HD] / own[HD : HD + 1] + text[0:HD] / text[HD : HD + 1])
-        att[pl.ds(pl.multiple_of(n * HD, 8), HD), :] = jnp.concatenate(made, axis=1)
+        tx_copy(which).start()
+    with jax.named_scope("queries"):
+        lax.fori_loop(0, 2, one_query_block, 0)
+    with jax.named_scope("partner"):
+        for which in range(2):
+            tx_wait(which)
+            for pair in range(4):
+                kv_wait(pair, which)
+
+    def scores(n, keys, dst, rows, cols):
+        dst[rows, cols] = jnp.exp2(nn(q[n, rows, 0:HP], keys)).astype(BF)
+
+    halves = (slice(0, 256), slice(256, 512))
+    own_cols = [slice(256 * k, 256 * k + 256) for k in range(8)]
+    text_cols = slice(2048, 2048 + TXT)
+
+    def stage(ahead, dst, behind, src):
+        made = [None, None]
+        for cols in own_cols:
+            for k, rows in enumerate(halves):
+                if ahead is not None:
+                    scores(ahead, kT[ahead, :, cols], dst, rows, cols)
+                if behind is not None:
+                    term = nt(vT[behind, :, cols], src[rows, cols])
+                    made[k] = term if made[k] is None else made[k] + term
+        if ahead is not None:
+            scores(ahead, tk[ahead], dst, slice(0, 512), text_cols)
+        if behind is not None:
+            own = jnp.concatenate(made, axis=1)
+            text = nt(tv[behind], src[:, text_cols])
+            total = own[0:HD] / own[HD : HD + 1] + text[0:HD] / text[HD : HD + 1]
+            att[pl.ds(pl.multiple_of(behind * HD, 8), HD), :] = total
+
+    def two_heads(n, carry):
+        stage(2 * n + 1, p_odd, 2 * n, p_even)
+        stage(2 * n + 2, p_even, 2 * n + 1, p_odd)
         return carry
 
-    lax.fori_loop(0, H, one_head, 0)
+    with jax.named_scope("attention"):
+        stage(0, p_even, None, None)
+        lax.fori_loop(0, H // 2 - 1, two_heads, 0)
+        stage(H - 1, p_odd, H - 2, p_even)
+        stage(None, None, H - 1, p_odd)
 
     attb[...] = att[...].astype(BF)
     for t in range(4):
@@ -537,10 +576,11 @@
             def _(which=which, t=t):
                 out_copy(which, t).wait_send()
 
-    for which, count in ((0, 4), (1, 3)):
-        for n in range(count):
-            dst = out.at[which, n]
-            pltpu.make_async_copy(dst, dst, out_recv.at[which, n]).wait()
+    with jax.named_scope("arrivals"):
+        for which, count in ((0, 4), (1, 3)):
+            for n in range(count):
+                dst = out.at[which, n]
+                pltpu.make_async_copy(dst, dst, out_recv.at[which, n]).wait()
 
     @pl.when(qd < 15)
     def _():
@@ -583,6 +623,8 @@
             pltpu.VMEM((H, HP, 2048), BF),
             pltpu.VMEM((H, HP, 2048), BF),
             pltpu.VMEM((H, 512, 128), BF),
+            pltpu.VMEM((512, 2048 + TXT), BF),
+            pltpu.VMEM((512, 2048 + TXT), BF),
             pltpu.VMEM((H, HP, TXT), BF),
             pltpu.VMEM((H, HP, TXT), BF),
             pltpu.VMEM((D, 512), F32),

time: 79.5 us -> 71.5 us (0.90)
  Pallas kernels: 77 us -> 69.2 us
    pallas_call x1, Pallas kernels: 77 us -> 69.2 us  [body(): pl.pallas_call(kernel, out_shape=jax.ShapeDtypeStruct((2,) + latents.shap...]
where the time goes in v3:
time: 71.5 us; the launch traced here: 71.3 us
  Pallas kernels  69.2 us (97%)
  local copies, waits for them, and re-layouts  1.4 us (2%)
    pallas_call x1, Pallas kernels, body(): pl.pallas_call(kernel, out_shape=jax.ShapeDtypeStruct((2,) + latents.shap...  69.2 us

profile of v3, /device:TPU:49, one launch (start us, length us, event | category | flops | bytes accessed | tf_op | source)
XLA Modules:
  0.0 71.3 jit_solution(3357094321102193702)
XLA Ops:
  0.6 69.2 %denoise.1 = f32[2,4,16,128]{3,2,1,0:T(8,128)} custom-call(f32[4,16,128]{2,1,0:T(8,128)} %latents.1, s32[4]{0:T(128)} %steps.1, bf16[128,1152]{1,0:T(8,128)(2,1)} %posin.1, bf16[9,16,128]{2,1,0:T(8,128)(2,1)} %bitcast.13, f32[5,30,1152]{2,1,0:T(8,128)} %bitcast.12, f32[1,31]{1,0:T(1,128)} %bitcast.15, f32[1,72]{1,0:T(1,128)} %bitcast.16, f32[1,72]{1,0:T(1,128)} %bitcast.17, ...), custom_call_target="tpu_custom_call" | custom-call | tf_op jit(solution)/shard_map/denoise/pallas_call | solution.py:604
  69.9 1.4 %slice_bitcast_fusion = (f32[4,16,128]{2,1,0:T(8,128)}, f32[4,16,128]{2,1,0:T(8,128)}) fusion(f32[2,4,16,128]{3,2,1,0:T(8,128)} %denoise.1), kind=kLoop, calls=%fused_computation | loop fusion | bytes 131072 | tf_op jit(solution)/shard_map/squeeze | solution.py:656

commit v4 on v3

--- a/solution.py
+++ b/solution.py
@@ -398,6 +398,14 @@
             weights(0).wait()
             turn(wqkv, wt, 0, 9)
 
+        @pl.when(row == part)
+        def _():
+            for k in range(2):
+                slot = pair * 2 + k
+                cols = pl.ds(pl.multiple_of((lax.rem(pair, 2) * 2 + k) * 128, 128), 128)
+                places = pos[slot, 0:TXT].T.astype(F32)
+                hid[:, cols] = tn(e3[...], split3(lat[slot, 0:C])) + places
+
         @pl.when(n == 1)
         def _():
             weights(3).wait()
@@ -478,9 +486,6 @@
         stage(None, None, H - 1, p_odd)
 
     attb[...] = att[...].astype(BF)
-    for t in range(4):
-        slot = part * 4 + t
-        hid[:, t * 128 : t * 128 + 128] = tn(e3[...], split3(lat[slot, 0:C])) + pos[slot, 0:TXT].T.astype(F32)
     for g in range(2):
         r = slice(g * 576, g * 576 + 576)
         hid[r, :] = hid[r, :] + modsT[r, 2:3] * nn(wot[r, :], attb[...])

time: 71.5 us -> 71.5 us (level)
  no operation moved by 1% of the time
where the time goes in v4:
time: 71.5 us; the launch traced here: 71.3 us
  Pallas kernels  69.3 us (97%)
  local copies, waits for them, and re-layouts  1.4 us (2%)
    pallas_call x1, Pallas kernels, body(): pl.pallas_call(kernel, out_shape=jax.ShapeDtypeStruct((2,) + latents.shap...  69.3 us

profile of v4, /device:TPU:49, one launch (start us, length us, event | category | flops | bytes accessed | tf_op | source)
XLA Modules:
  0.0 71.3 jit_solution(7674481783559124949)
XLA Ops:
  0.6 69.3 %denoise.1 = f32[2,4,16,128]{3,2,1,0:T(8,128)} custom-call(f32[4,16,128]{2,1,0:T(8,128)} %latents.1, s32[4]{0:T(128)} %steps.1, bf16[128,1152]{1,0:T(8,128)(2,1)} %posin.1, bf16[9,16,128]{2,1,0:T(8,128)(2,1)} %bitcast.13, f32[5,30,1152]{2,1,0:T(8,128)} %bitcast.12, f32[1,31]{1,0:T(1,128)} %bitcast.15, f32[1,72]{1,0:T(1,128)} %bitcast.16, f32[1,72]{1,0:T(1,128)} %bitcast.17, ...), custom_call_target="tpu_custom_call" | custom-call | tf_op jit(solution)/shard_map/denoise/pallas_call | solution.py:609
  69.9 1.4 %slice_bitcast_fusion = (f32[4,16,128]{2,1,0:T(8,128)}, f32[4,16,128]{2,1,0:T(8,128)}) fusion(f32[2,4,16,128]{3,2,1,0:T(8,128)} %denoise.1), kind=kLoop, calls=%fused_computation | loop fusion | bytes 131072 | tf_op jit(solution)/shard_map/squeeze | solution.py:661
